TPU v7x, 32 devices: a whole 2x2x4 slice. The times are simulated.
32 devices in a mesh: dp: 4 (over y, core), ctx: 2 (over x), tensor: 4 (over z).
Axes of the slice: x: 2, y: 2, z: 4, core: 2. Of those that a mesh axis runs over, the one named last changes fastest.
Arguments:
- layer_input: bfloat16 [4, 512, 8192], P('dp', ('ctx', 'tensor')), may hold values from -6 to 6
- queries: bfloat16 [4, 512, 8192], P('dp', 'ctx', 'tensor'), may hold values from -12 to 12
- forward_output: bfloat16 [4, 512, 8192], P('dp', 'ctx', 'tensor'), may hold values from -6 to 6
- attention_output_gradient: bfloat16 [4, 512, 8192], P('dp', 'ctx', 'tensor'), may hold values from -6 to 6
- key_weight: bfloat16 [8192, 1024], P(None, 'tensor'), may hold values from -3 to 3
- value_projection_weight: bfloat16 [8192, 1024], P(None, 'tensor'), may hold values from -0.0625 to 0.0625
- segment: int32 [4, 512], P('dp'), may hold values from 0 to 4, as said below
- block_table: int32 [4, 4, 4], P('dp'), may hold values from 0 to 1, as said below
- block_owner: int32 [4, 4], P('dp'), may hold values from 0 to 3, each once within a row
Outputs:
- query_grad: bfloat16 [4, 512, 8192], P('dp', 'ctx', 'tensor')
- input_grad: bfloat16 [4, 512, 8192], P('dp', ('ctx', 'tensor'))
- key_weight_grad: bfloat16 [8192, 1024], P(('dp', 'ctx'), 'tensor')
- value_weight_grad: bfloat16 [8192, 1024], P(('dp', 'ctx'), 'tensor')
Inputs may be any that keep to these rules, and one draw needn't show every extreme that they name: Along the logical positions of a group the segment never falls; the prompt (0) comes first and every rollout 1 to 4 is present. block_table[g, b, c] is 1 only where some position of logical block b may read some position of logical block c under the causal and segment rule; block_table[g, b, b] is 1 for every block; other such pairs may be 0. `block_owner`: each group's row holds every logical block once.
All inputs are finite; a program needn't handle non-finite values.
Results may differ from a plain program's by a relative error of at most 0.005.
The roundings to bfloat16 on the way count: a program that leaves them out, or rounds other values in their place, can miss the bound.
Values may be sent and summed in bfloat16 or wider, within the bound.
A program may use at most 128 MiB of HBM per device.

v0:
```python
import math
import jax
import jax.numpy as jnp
from jax import lax
from jax.sharding import PartitionSpec as P

HEAD_SIZE = 128
BLK = 128


def per_device(
    layer_input,
    queries,
    forward_output,
    attention_output_gradient,
    key_weight,
    value_projection_weight,
    segment,
    block_table,
    block_owner,
):
    softmax_scale = 1.0 / math.sqrt(HEAD_SIZE)
    local_rows = queries.shape[1]
    kv_local = key_weight.shape[1] // HEAD_SIZE
    q_local = queries.shape[2] // HEAD_SIZE
    queries_per_group = q_local // kv_local
    kv_width = kv_local * HEAD_SIZE
    gathered = lax.all_gather(layer_input, "tensor", axis=1, tiled=True)[0]
    planes = lax.axis_size("tensor")
    plane_size = lax.axis_size("dp") * lax.axis_size("ctx")
    plane_index = lax.axis_index("dp") * lax.axis_size("ctx") + lax.axis_index("ctx")
    model_width = key_weight.shape[0]
    piece_rows = model_width // (planes * plane_size)

    def piece(weight):
        split = weight.reshape(planes, plane_size, piece_rows, kv_width)
        return lax.dynamic_index_in_dim(split, plane_index, 1, keepdims=False)

    pieces = jnp.concatenate([piece(key_weight), piece(value_projection_weight)], axis=2)
    pieces = lax.all_to_all(pieces, "tensor", split_axis=0, concat_axis=0, tiled=True)
    wide_weight = lax.all_gather(pieces, ("dp", "ctx"), axis=1, tiled=True)
    plane_input = lax.all_to_all(gathered, ("dp", "ctx"), split_axis=1, concat_axis=0, tiled=True)
    projected_keys = jnp.dot(gathered, key_weight, preferred_element_type=jnp.float32)
    projected_values = jnp.dot(
        gathered, value_projection_weight, preferred_element_type=jnp.float32
    )
    kv_rows = jnp.concatenate([projected_keys, projected_values], axis=1).astype(jnp.bfloat16)
    owner_row = block_owner[0]
    segments_row = segment[0]
    table_row = block_table[0]
    blocks_here = local_rows // BLK
    ctx_index = lax.axis_index("ctx")
    own_blocks = lax.dynamic_slice_in_dim(owner_row, ctx_index * blocks_here, blocks_here)
    offsets = jnp.arange(BLK, dtype=jnp.int32)
    query_pos = (own_blocks[:, None] * BLK + offsets[None, :]).reshape(-1)
    query_seg = jnp.take(segments_row, query_pos)
    own_table = jnp.take(table_row, own_blocks, axis=0)
    query_heads = queries[0].reshape(local_rows, kv_local, queries_per_group, HEAD_SIZE)
    grad_heads = attention_output_gradient[0].reshape(
        local_rows, kv_local, queries_per_group, HEAD_SIZE
    )
    saved_heads = forward_output[0].reshape(local_rows, kv_local, queries_per_group, HEAD_SIZE)
    correction = jnp.sum(grad_heads.astype(jnp.float32) * saved_heads.astype(jnp.float32), axis=-1)
    correction = correction.transpose(1, 2, 0)

    def allowed_for(leading_row, row_count):
        key_blocks = lax.dynamic_slice_in_dim(owner_row, leading_row // BLK, row_count // BLK)
        key_pos = (key_blocks[:, None] * BLK + offsets[None, :]).reshape(-1)
        key_seg = jnp.take(segments_row, key_pos)
        table_part = jnp.take(own_table, key_blocks, axis=1) == 1
        table_full = jnp.broadcast_to(
            table_part[:, None, :, None], (blocks_here, BLK, row_count // BLK, BLK)
        )
        table_full = table_full.reshape(local_rows, row_count)
        same_tree = (key_seg[None, :] == 0) | (key_seg[None, :] == query_seg[:, None])
        return table_full & (key_pos[None, :] <= query_pos[:, None]) & same_tree

    def block_scores(block_rows, leading_row):
        row_count = block_rows.shape[0]
        block_keys = block_rows[:, :kv_width].reshape(row_count, kv_local, HEAD_SIZE)
        block_values = block_rows[:, kv_width:].reshape(row_count, kv_local, HEAD_SIZE)
        raw_scores = (
            jnp.einsum(
                "qhgd,khd->hgqk", query_heads, block_keys, preferred_element_type=jnp.float32
            )
            * softmax_scale
        )
        allowed = allowed_for(leading_row, row_count)
        return (jnp.where(allowed[None, None], raw_scores, -jnp.inf), block_keys, block_values)

    def stats_block(carried, block_rows, leading_row):
        running_max, running_sum = carried
        scores = block_scores(block_rows, leading_row)[0]
        new_max = jnp.maximum(running_max, jnp.max(scores, axis=-1))
        running_sum = running_sum * jnp.exp(running_max - new_max) + jnp.sum(
            jnp.exp(scores - new_max[..., None]), axis=-1
        )
        return (new_max, running_sum)

    def grads_block(carried, block_rows, leading_row, log_norm):
        query_sum, keyval_sum = carried
        row_count = block_rows.shape[0]
        scores, block_keys, block_values = block_scores(block_rows, leading_row)
        probabilities = jnp.exp(scores - log_norm[..., None])
        probs_low = probabilities.astype(jnp.bfloat16)
        value_gradient_rows = jnp.einsum(
            "hgqk,qhgd->khd", probs_low, grad_heads, preferred_element_type=jnp.float32
        )
        prob_grads = jnp.einsum(
            "qhgd,khd->hgqk", grad_heads, block_values, preferred_element_type=jnp.float32
        )
        score_low = (probabilities * (prob_grads - correction[..., None])).astype(jnp.bfloat16)
        query_sum = query_sum + jnp.einsum(
            "hgqk,khd->qhgd", score_low, block_keys, preferred_element_type=jnp.float32
        )
        key_gradient_rows = (
            jnp.einsum("hgqk,qhgd->khd", score_low, query_heads, preferred_element_type=jnp.float32)
            * softmax_scale
        )
        update = jnp.concatenate(
            [
                key_gradient_rows.reshape(row_count, kv_width),
                value_gradient_rows.reshape(row_count, kv_width),
            ],
            axis=1,
        )
        keyval_sum = lax.dynamic_update_slice_in_dim(keyval_sum, update, leading_row, 0)
        return (query_sum, keyval_sum)

    def over_blocks(block_step, carried, shard_part):
        row_count = shard_part.shape[0]
        block_size = math.gcd(row_count, max(512, local_rows))
        block_count = row_count // block_size
        pieces = shard_part.reshape(block_count, block_size, shard_part.shape[1])
        starts = block_size * jnp.arange(block_count, dtype=jnp.int32)

        def one_block(state_in, scan_item):
            block_rows, block_start = scan_item
            result = block_step(state_in, block_rows, block_start)
            return (result, None)

        carried, _ = lax.scan(one_block, carried, (pieces, starts))
        return carried

    stats_init = (
        jnp.full((kv_local, queries_per_group, local_rows), -1e30, jnp.float32),
        jnp.zeros((kv_local, queries_per_group, local_rows), jnp.float32),
    )
    seq_rows = local_rows * lax.axis_size("ctx")
    grads_init = (
        jnp.zeros((local_rows, kv_local, queries_per_group, HEAD_SIZE), jnp.float32),
        jnp.zeros((seq_rows, 2 * kv_width), jnp.float32),
    )
    running_max, running_sum = over_blocks(
        stats_block, stats_init, lax.all_gather(kv_rows, "ctx", axis=0, tiled=True)
    )
    log_norm = running_max + jnp.log(running_sum)

    def grads_fold(carried, shard_part):
        return over_blocks(
            lambda state, rows_in, start_in: grads_block(state, rows_in, start_in, log_norm),
            carried,
            shard_part,
        )

    query_sum, keyval_sum = grads_fold(
        grads_init, lax.all_gather(kv_rows, "ctx", axis=0, tiled=True)
    )
    own_grads = lax.psum_scatter(keyval_sum, "ctx", scatter_dimension=0, tiled=True).astype(
        jnp.bfloat16
    )
    query_grad = (
        (query_sum * softmax_scale).astype(jnp.bfloat16).reshape(1, local_rows, q_local * HEAD_SIZE)
    )
    kv_all = lax.all_gather(own_grads, "tensor", axis=0)
    kv_plane = lax.all_gather(own_grads, ("dp", "ctx"), axis=0, tiled=True)
    width_part = lax.dot_general(
        kv_all, wide_weight, (((0, 2), (0, 2)), ((), ())), preferred_element_type=jnp.float32
    ).astype(jnp.bfloat16)
    input_grad = lax.all_to_all(width_part, "tensor", split_axis=0, concat_axis=1, tiled=True)[None]
    weight_sum = lax.dot_general(
        plane_input, kv_plane, (((0,), (0,)), ((), ())), preferred_element_type=jnp.float32
    )
    key_weight_grad = weight_sum[:, :kv_width].astype(jnp.bfloat16)
    value_weight_grad = weight_sum[:, kv_width:].astype(jnp.bfloat16)
    return (query_grad, input_grad, key_weight_grad, value_weight_grad)


def solution(mesh):
    in_specs = (
        P("dp", ("ctx", "tensor"), None),
        P("dp", "ctx", "tensor"),
        P("dp", "ctx", "tensor"),
        P("dp", "ctx", "tensor"),
        P(None, "tensor"),
        P(None, "tensor"),
        P("dp", None),
        P("dp", None, None),
        P("dp", None),
    )
    out_specs = (
        P("dp", "ctx", "tensor"),
        P("dp", ("ctx", "tensor"), None),
        P(("dp", "ctx"), "tensor"),
        P(("dp", "ctx"), "tensor"),
    )
    return jax.shard_map(
        per_device, mesh=mesh, in_specs=in_specs, out_specs=out_specs, check_vma=False
    )
```

profile of v0, /device:TPU:0, one launch (start us, length us, event | category | flops | bytes accessed | tf_op | source)
XLA Modules:
  0.0 300.7 jit_solution(7361246667366215008)
XLA Ops:
  13.8 1.9 gather_fusion.1
  15.8 3.5 %gather_fusion.3 = s32[512]{0:T(512)S(1)} fusion(s32[512]{0:T(512)S(1)} %bitcast.138, s32[1024]{0:T(1024)S(1)} %pad_clamp_fusion.1), kind=kCustom, calls=%fused_computation.1.clone | custom fusion | bytes 6144 | tf_op jit(solution)/shard_map/while/body/eval_jaxpr/jit(_take)/gather | solution.py:69
  20.8 1.5 copy.108
  22.2 1.6 copy.82
  25.4 67.6 %all-gather.6.cloned.1.call-done = bf16[1,256,8192]{2,1,0:T(8,128)(2,1)} async-done(((bf16[1,64,8192]{2,1,0:T(8,128)(2,1)}), bf16[1,256,8192]{2,1,0:T(8,128)(2,1)}) %all-gather.6.cloned.1.call-update) | async-done | bytes 4194320 | tf_op jit(solution)/shard_map/all_gather | solution.py:28
  93.1 5.3 %fusion.14 = bf16[256,256]{0,1:T(8,128)(2,1)S(1)} fusion(bf16[8192,256]{1,0:T(8,128)(2,1)} %param.17, bf16[1,256,8192]{2,1,0:T(8,128)(2,1)} %all-gather.6.cloned.1.call-done), kind=kOutput, calls=%fused_computation.27 | convolution fusion | flops 1073807360 | bytes 8519680 | tf_op jit(solution)/shard_map/dot_general | solution.py:43
  99.0 1.9 fusion.17
  100.9 8.9 %all_gather.20 = bf16[512,512]{0,1:T(8,128)(2,1)S(1)} all-gather(bf16[256,512]{0,1:T(8,128)(2,1)S(1)} %pad_maximum_fusion.2), channel_id=1, replica_groups=mesh['dp'=4,'ctx'=2,'tensor'=4] {'ctx'}, dimensions={0}, use_global_device_ids=true | all-gather | bytes 786432 | tf_op jit(solution)/shard_map/all_gather | solution.py:167
  109.9 1.4 fusion.3
  111.3 1.7 exponential_reduce_fusion
  113.0 2.3 fusion.8
  115.3 2.9 fusion.1
  118.2 2.0 copy-done.3
  120.2 1.5 fusion.13
  122.7 1.3 dynamic-slice_bitcast_fusion
  125.1 3.6 %all-to-all-start = ((bf16[4,256,512]{2,1,0:T(8,128)(2,1)}), bf16[4,256,512]{2,1,0:T(8,128)(2,1)S(1)}, u32[]{:S(2)}, u32[]{:S(2)}) async-start(bf16[4,256,512]{2,1,0:T(8,128)(2,1)} %pad_maximum_fusion.1), calls=%async_computation.1 | async-start | bytes 2097152 | tf_op jit(solution)/shard_map/all_to_all | solution.py:40
  128.7 13.1 %reduce-scatter.2.cloned.1.call-done = f32[256,512]{0,1:T(8,128)} async-done(((f32[512,512]{0,1:T(8,128)}), f32[256,512]{0,1:T(8,128)}) %reduce-scatter.2.cloned.1.call-update) | async-done | bytes 524304 | tf_op jit(solution)/shard_map/reduce_scatter | solution.py:169
  141.8 1.8 convert_element_type.47
  143.7 10.1 %all-to-all-done = bf16[4,256,512]{2,1,0:T(8,128)(2,1)S(1)} async-done(((bf16[4,256,512]{2,1,0:T(8,128)(2,1)}), bf16[4,256,512]{2,1,0:T(8,128)(2,1)S(1)}, u32[]{:S(2)}, u32[]{:S(2)}) %all-to-all-start) | async-done | bytes 1048608 | tf_op jit(solution)/shard_map/all_to_all | solution.py:40
  154.7 6.4 %copy.87 = bf16[1,256,8192]{1,2,0:T(8,128)(2,1)} copy(bf16[1,256,8192]{2,1,0:T(8,128)(2,1)} %all-gather.6.cloned.1.call-done) | data formatting | bytes 8388608 | tf_op jit(solution)/shard_map/all_gather | solution.py:28
  161.1 4.6 %all-to-all-start.2 = ((bf16[256,8,1024]{0,2,1:T(8,128)(2,1)}), bf16[256,8,1024]{0,2,1:T(8,128)(2,1)}, u32[]{:S(2)}, u32[]{:S(2)}) async-start(bf16[256,8,1024]{0,2,1:T(8,128)(2,1)} %bitcast.140), calls=%async_computation.3 | async-start | bytes 8388608 | tf_op jit(solution)/shard_map/all_to_all | solution.py:42
  166.3 8.0 %all-gather.12.cloned.1.call-done = bf16[1024,512]{0,1:T(8,128)(2,1)} async-done(((bf16[256,512]{0,1:T(8,128)(2,1)}), bf16[1024,512]{0,1:T(8,128)(2,1)}) %all-gather.12.cloned.1.call-update) | async-done | bytes 1048592 | tf_op jit(solution)/shard_map/all_gather | solution.py:175
  174.3 1.5 copy.83
  175.8 78.1 %all-gather.8.cloned.1.call-done = bf16[4,2048,512]{2,1,0:T(8,128)(2,1)} async-done(((bf16[4,256,512]{2,1,0:T(8,128)(2,1)}), bf16[4,2048,512]{2,1,0:T(8,128)(2,1)}) %all-gather.8.cloned.1.call-update) | async-done | bytes 8388624 | tf_op jit(solution)/shard_map/all_gather | solution.py:41
  253.9 6.7 %fusion.11 = bf16[256,2048]{1,0:T(8,128)(2,1)} fusion(bf16[4,256,512]{2,1,0:T(8,128)(2,1)S(1)} %bitcast.155, bf16[4,2048,512]{2,1,0:T(8,128)(2,1)} %all-gather.8.cloned.1.call-done), kind=kOutput, calls=%fused_computation.19 | convolution fusion | flops 2148007936 | bytes 10485760 | tf_op jit(solution)/shard_map/dot_general | solution.py:177
  260.6 4.6 %all-to-all-start.1 = ((bf16[4,64,2048]{2,1,0:T(8,128)(2,1)}), bf16[4,64,2048]{2,1,0:T(8,128)(2,1)S(1)}, u32[]{:S(2)}, u32[]{:S(2)}) async-start(bf16[4,64,2048]{2,1,0:T(8,128)(2,1)} %bitcast.37), calls=%async_computation.2 | async-start | bytes 2097152 | tf_op jit(solution)/shard_map/all_to_all | solution.py:180
  265.2 2.9 multiply_convert_fusion
  268.1 1.4 copy.89
  269.5 6.4 %copy.88 = bf16[8,256,1024]{2,1,0:T(8,128)(2,1)} copy(bf16[8,256,1024]{1,2,0:T(8,128)(2,1)} %bitcast.40) | data formatting | bytes 8388608 | tf_op jit(solution)/shard_map/all_to_all | solution.py:42
  276.0 8.6 %all-gather.10.cloned.1.call-done = bf16[2048,512]{0,1:T(8,128)(2,1)} async-done(((bf16[256,512]{0,1:T(8,128)(2,1)}), bf16[2048,512]{0,1:T(8,128)(2,1)}) %all-gather.10.cloned.1.call-update) | async-done | bytes 2097168 | tf_op jit(solution)/shard_map/all_gather | solution.py:176
  284.6 5.2 %fusion.12 = bf16[1024,512]{0,1:T(8,128)(2,1)S(1)} fusion(bf16[2048,512]{0,1:T(8,128)(2,1)} %all-gather.10.cloned.1.call-done, bf16[2048,1024]{1,0:T(8,128)(2,1)} %bitcast.148), kind=kOutput, calls=%fused_computation.24 | convolution fusion | flops 2148007936 | bytes 7340032 | tf_op jit(solution)/shard_map/dot_general | solution.py:181
  292.6 1.6 broadcast_in_dim.114
  (68 shorter events, 17.0 us)
Async XLA Ops:
  7.2 6.6 %copy-start = (s32[1,512]{1,0:T(1,128)S(1)}, s32[1,512]{1,0:T(1,128)}, u32[]{:S(2)}) copy-start(s32[1,512]{1,0:T(1,128)} %param.19) | copy-start | bytes 6148
  7.2 13.0 %copy-start.7 = (bf16[1,256,2048]{2,1,0:T(8,128)(2,1)S(1)}, bf16[1,256,2048]{2,1,0:T(8,128)(2,1)}, u32[]{:S(2)}) copy-start(bf16[1,256,2048]{2,1,0:T(8,128)(2,1)} %param.14) | copy-start | bytes 3145732
  7.2 85.9 %all-gather.6.cloned.1.call-start = ((), (), s32[]{:S(2)}) async-start(), calls=%async_computation.4 | async-start | bytes 5242880 | tf_op jit(solution)/shard_map/all_gather | solution.py:28
  7.9 133.9 %reduce-scatter.2.cloned.1.call-start = ((), (), s32[]{:S(2)}) async-start(), calls=%async_computation.5 | async-start | bytes 1572864 | tf_op jit(solution)/shard_map/reduce_scatter | solution.py:169
  15.8 8.0 %copy-start.6 = (bf16[1,256,2048]{2,1,0:T(8,128)(2,1)S(1)}, bf16[1,256,2048]{2,1,0:T(8,128)(2,1)}, u32[]{:S(2)}) copy-start(bf16[1,256,2048]{2,1,0:T(8,128)(2,1)} %param.15) | copy-start | bytes 3145732
  93.1 5.3 %copy-start.2 = (bf16[1,256,8192]{2,1,0:T(8,128)(2,1)S(1)}, bf16[1,256,8192]{2,1,0:T(8,128)(2,1)}, u32[]{:S(2)}) copy-start(bf16[1,256,8192]{2,1,0:T(8,128)(2,1)} %all-gather.6.cloned.1.call-done) | copy-start | bytes 12582916
  93.1 5.9 %copy-start.4 = (bf16[8192,256]{1,0:T(8,128)(2,1)S(1)}, bf16[8192,256]{1,0:T(8,128)(2,1)}, u32[]{:S(2)}) copy-start(bf16[8192,256]{1,0:T(8,128)(2,1)} %param.18) | copy-start | bytes 12582916
  111.3 1.8 copy-start.8
  118.2 2.0 copy-start.3
  125.1 28.6 %all-to-all-start = ((bf16[4,256,512]{2,1,0:T(8,128)(2,1)}), bf16[4,256,512]{2,1,0:T(8,128)(2,1)S(1)}, u32[]{:S(2)}, u32[]{:S(2)}) async-start(bf16[4,256,512]{2,1,0:T(8,128)(2,1)} %pad_maximum_fusion.1), calls=%async_computation.1 | async-start | bytes 2097152 | tf_op jit(solution)/shard_map/all_to_all | solution.py:40
  128.7 45.6 %all-gather.12.cloned.1.call-start = ((), (), s32[]{:S(2)}) async-start(), calls=%async_computation.8 | async-start | bytes 1310720 | tf_op jit(solution)/shard_map/all_gather | solution.py:175
  143.6 110.3 %all-gather.8.cloned.1.call-start = ((), (), s32[]{:S(2)}) async-start(), calls=%async_computation.6 | async-start | bytes 9437184 | tf_op jit(solution)/shard_map/all_gather | solution.py:41
  153.7 1.0 copy-start.5
  161.1 99.5 %all-to-all-start.2 = ((bf16[256,8,1024]{0,2,1:T(8,128)(2,1)}), bf16[256,8,1024]{0,2,1:T(8,128)(2,1)}, u32[]{:S(2)}, u32[]{:S(2)}) async-start(bf16[256,8,1024]{0,2,1:T(8,128)(2,1)} %bitcast.140), calls=%async_computation.3 | async-start | bytes 8388608 | tf_op jit(solution)/shard_map/all_to_all | solution.py:42
  165.7 118.9 %all-gather.10.cloned.1.call-start = ((), (), s32[]{:S(2)}) async-start(), calls=%async_computation.7 | async-start | bytes 2359296 | tf_op jit(solution)/shard_map/all_gather | solution.py:176
  260.6 31.2 %all-to-all-start.1 = ((bf16[4,64,2048]{2,1,0:T(8,128)(2,1)}), bf16[4,64,2048]{2,1,0:T(8,128)(2,1)S(1)}, u32[]{:S(2)}, u32[]{:S(2)}) async-start(bf16[4,64,2048]{2,1,0:T(8,128)(2,1)} %bitcast.37), calls=%async_computation.2 | async-start | bytes 2097152 | tf_op jit(solution)/shard_map/all_to_all | solution.py:180
  284.6 9.7 %copy-start.1 = (s32[1,512]{1,0:T(1,128)S(1)}, s32[1,512]{1,0:T(1,128)}, u32[]{:S(2)}) copy-start(s32[1,512]{1,0:T(1,128)} %param.19) | copy-start | bytes 6148
Sparse Core Ops, SparseCore 0:
  9.6 83.4 all-gather.5
  122.9 18.9 reduce-scatter.1
  144.0 30.2 all-gather.11
  176.8 77.0 all-gather.7
  256.3 28.1 all-gather.9
where the time goes:
time: 302 us; the launch traced here: 301 us
  waiting for transfers between devices  187 us (62%)
  local copies, waits for them, and re-layouts  37 us (12%)
  matrix products  30 us (10%)
  between operations  14.1 us (5%)
  starting transfers between devices  13 us (4%)
  other arithmetic  11.1 us (4%)
  blocking collectives  8.92 us (3%)
    all_gather x1, waiting for transfers between devices, per_device(): wide_weight = lax.all_gather(pieces, ('dp', 'ctx'), axis=1, tiled=True)  78.1 us
    all_gather x1, waiting for transfers between devices, per_device(): gathered = lax.all_gather(layer_input, 'tensor', axis=1, tiled=True)[0]  67.6 us
    reduce_scatter x1, waiting for transfers between devices, per_device(): lax.psum_scatter(keyval_sum, 'ctx', scatter_dimension=0, tiled=True)  13.1 us
    all_to_all x1, waiting for transfers between devices, per_device(): lax.all_to_all(pieces, 'tensor', split_axis=0, concat_axis=0, tiled=True)  10.1 us
    all_gather x1, blocking collectives, per_device(): lax.all_gather(kv_rows, 'ctx', axis=0, tiled=True)  8.92 us
    unnamed x23, local copies, waits for them, and re-layouts  8.82 us
    all_gather x1, waiting for transfers between devices, per_device(): kv_plane = lax.all_gather(own_grads, ('dp', 'ctx'), axis=0, tiled=True)  8.59 us
    all_gather x1, waiting for transfers between devices, per_device(): kv_all = lax.all_gather(own_grads, 'tensor', axis=0)  7.99 us
  transfers between devices with their start and end apart: 8, of which 6 were waited for; matrix products, arithmetic and copies ran while one was open for 18% of the time, Pallas kernels for 0%

commit v1 on v0

--- a/solution.py
+++ b/solution.py
@@ -39,7 +39,15 @@
     pieces = jnp.concatenate([piece(key_weight), piece(value_projection_weight)], axis=2)
     pieces = lax.all_to_all(pieces, "tensor", split_axis=0, concat_axis=0, tiled=True)
     wide_weight = lax.all_gather(pieces, ("dp", "ctx"), axis=1, tiled=True)
-    plane_input = lax.all_to_all(gathered, ("dp", "ctx"), split_axis=1, concat_axis=0, tiled=True)
+    plane_input = jnp.concatenate(
+        lax.all_to_all(
+            jnp.stack(jnp.split(gathered, lax.axis_size(("dp", "ctx")), axis=1)),
+            ("dp", "ctx"),
+            0,
+            0,
+        ),
+        axis=0,
+    )
     projected_keys = jnp.dot(gathered, key_weight, preferred_element_type=jnp.float32)
     projected_values = jnp.dot(
         gathered, value_projection_weight, preferred_element_type=jnp.float32

time: 302 us -> 306 us (1.013)
  waiting for transfers between devices: 187 us -> 194 us
    unnamed x23 -> x30, local copies, waits for them, and re-layouts: 8.82 us -> 17.1 us
    all_gather x1, waiting for transfers between devices: 8.59 us -> 15 us  [per_device(): kv_plane = lax.all_gather(own_grads, ('dp', 'ctx'), axis=0, tiled=True)]
    all_to_all x1 -> x0, local copies, waits for them, and re-layouts: 6.44 us -> none  [per_device(): lax.all_to_all(gathered, ('dp', 'ctx'), split_axis=1, concat_axis=0, tile...]
    all_gather x1 -> x0, local copies, waits for them, and re-layouts: 6.36 us -> none  [per_device(): gathered = lax.all_gather(layer_input, 'tensor', axis=1, tiled=True)[0]]
    all_gather x1, waiting for transfers between devices: 78.1 us -> 82.8 us  [per_device(): wide_weight = lax.all_gather(pieces, ('dp', 'ctx'), axis=1, tiled=True)]
    all_gather x1, waiting for transfers between devices: 7.99 us -> 3.26 us  [per_device(): kv_all = lax.all_gather(own_grads, 'tensor', axis=0)]
    dot_general x1, matrix products: 5.33 us -> 1.86 us  [per_device(): jnp.dot(gathered, key_weight, preferred_element_type=jnp.float32)]
    dot_general x1, matrix products: 1.86 us -> 5.33 us  [per_device(): jnp.dot(gathered, value_projection_weight, preferred_element_type=jnp.flo...]
  transfers between devices with their start and end apart: 8 -> 8, of which waited for: 6 -> 7; matrix products, arithmetic and copies ran while one was open for 18% -> 17% of each run, Pallas kernels for 0% -> 0%
where the time goes in v1:
time: 306 us; the launch traced here: 305 us
  waiting for transfers between devices  194 us (63%)
  local copies, waits for them, and re-layouts  34.2 us (11%)
  matrix products  30.1 us (10%)
  between operations  14.1 us (5%)
  starting transfers between devices  13 us (4%)
  other arithmetic  11.1 us (4%)
  blocking collectives  8.92 us (3%)
    all_gather x1, waiting for transfers between devices, per_device(): wide_weight = lax.all_gather(pieces, ('dp', 'ctx'), axis=1, tiled=True)  82.8 us
    all_gather x1, waiting for transfers between devices, per_device(): gathered = lax.all_gather(layer_input, 'tensor', axis=1, tiled=True)[0]  67.7 us
    unnamed x30, local copies, waits for them, and re-layouts  17.1 us
    all_gather x1, waiting for transfers between devices, per_device(): kv_plane = lax.all_gather(own_grads, ('dp', 'ctx'), axis=0, tiled=True)  15 us
    reduce_scatter x1, waiting for transfers between devices, per_device(): lax.psum_scatter(keyval_sum, 'ctx', scatter_dimension=0, tiled=True)  13.1 us
    all_to_all x1, waiting for transfers between devices, per_device(): lax.all_to_all(pieces, 'tensor', split_axis=0, concat_axis=0, tiled=True)  10.1 us
    all_gather x1, blocking collectives, per_device(): lax.all_gather(kv_rows, 'ctx', axis=0, tiled=True)  8.92 us
    dot_general x1, matrix products, per_device(): lax.dot_general(kv_all, wide_weight, (((0, 2), (0, 2)), ((), ())), prefer...  6.71 us
  transfers between devices with their start and end apart: 8, of which 7 were waited for; matrix products, arithmetic and copies ran while one was open for 17% of the time, Pallas kernels for 0%

profile of v1, /device:TPU:0, one launch (start us, length us, event | category | flops | bytes accessed | tf_op | source)
XLA Modules:
  0.0 305.0 jit_solution(4992728812437884992)
XLA Ops:
  13.8 1.9 gather_fusion.1
  15.8 3.5 %gather_fusion.3 = s32[512]{0:T(512)S(1)} fusion(s32[512]{0:T(512)S(1)} %bitcast.162, s32[1024]{0:T(1024)S(1)} %get-tuple-element.106), kind=kCustom, calls=%fused_computation.1.clone | custom fusion | bytes 6144 | tf_op jit(solution)/shard_map/while/body/eval_jaxpr/jit(_take)/gather | solution.py:77
  20.7 1.5 copy.79
  22.2 1.6 copy.57
  25.4 67.7 %all-gather.6.cloned.1.call-done = bf16[1,256,8192]{2,1,0:T(8,128)(2,1)} async-done(((bf16[1,64,8192]{2,1,0:T(8,128)(2,1)}), bf16[1,256,8192]{2,1,0:T(8,128)(2,1)}) %all-gather.6.cloned.1.call-update) | async-done | bytes 4194320 | tf_op jit(solution)/shard_map/all_gather | solution.py:28
  93.1 5.3 %convolution_convert_fusion.1 = bf16[256,256]{0,1:T(8,128)(2,1)S(1)} fusion(bf16[8192,256]{1,0:T(8,128)(2,1)} %param.18, bf16[1,256,8192]{2,1,0:T(8,128)(2,1)} %all-gather.6.cloned.1.call-done), kind=kOutput, calls=%fused_computation.22 | convolution fusion | flops 1073807360 | bytes 8519680 | tf_op jit(solution)/shard_map/dot_general | solution.py:52
  99.0 1.9 convolution_convert_fusion.2
  100.9 8.9 %all_gather.20 = bf16[512,512]{0,1:T(8,128)(2,1)S(1)} all-gather(bf16[256,512]{0,1:T(8,128)(2,1)S(1)} %pad_maximum_fusion.2), channel_id=1, replica_groups=mesh['dp'=4,'ctx'=2,'tensor'=4] {'ctx'}, dimensions={0}, use_global_device_ids=true | all-gather | bytes 786432 | tf_op jit(solution)/shard_map/all_gather | solution.py:175
  111.3 1.7 exponential_reduce_fusion
  113.0 2.3 fusion.4
  115.3 2.9 fusion.1
  118.2 2.0 copy-done.4
  120.2 1.5 fusion.8
  125.1 3.6 %all-to-all-start = ((bf16[4,256,512]{2,1,0:T(8,128)(2,1)}), bf16[4,256,512]{2,1,0:T(8,128)(2,1)S(1)}, u32[]{:S(2)}, u32[]{:S(2)}) async-start(bf16[4,256,512]{2,1,0:T(8,128)(2,1)} %pad_maximum_fusion.1), calls=%async_computation.1 | async-start | bytes 2097152 | tf_op jit(solution)/shard_map/all_to_all | solution.py:40
  128.7 13.1 %reduce-scatter.2.cloned.1.call-done = f32[256,512]{0,1:T(8,128)} async-done(((f32[512,512]{0,1:T(8,128)}), f32[256,512]{0,1:T(8,128)}) %reduce-scatter.2.cloned.1.call-update) | async-done | bytes 524304 | tf_op jit(solution)/shard_map/reduce_scatter | solution.py:177
  141.8 1.8 convert_element_type.47
  143.7 10.1 %all-to-all-done = bf16[4,256,512]{2,1,0:T(8,128)(2,1)S(1)} async-done(((bf16[4,256,512]{2,1,0:T(8,128)(2,1)}), bf16[4,256,512]{2,1,0:T(8,128)(2,1)S(1)}, u32[]{:S(2)}, u32[]{:S(2)}) %all-to-all-start) | async-done | bytes 1048608 | tf_op jit(solution)/shard_map/all_to_all | solution.py:40
  154.7 2.0 fusion.16
  156.8 1.9 fusion.15
  158.7 1.9 fusion.14
  160.5 1.9 fusion.13
  165.8 4.6 %all-to-all-start.2 = ((bf16[8,256,1024]{2,1,0:T(8,128)(2,1)}), bf16[8,256,1024]{2,1,0:T(8,128)(2,1)}, u32[]{:S(2)}, u32[]{:S(2)}) async-start(bf16[8,256,1024]{2,1,0:T(8,128)(2,1)} %fusion.9), calls=%async_computation.3 | async-start | bytes 8388608 | tf_op jit(solution)/shard_map/all_to_all | solution.py:43
  171.0 3.3 %all-gather.12.cloned.1.call-done = bf16[1024,512]{0,1:T(8,128)(2,1)} async-done(((bf16[256,512]{0,1:T(8,128)(2,1)}), bf16[1024,512]{0,1:T(8,128)(2,1)}) %all-gather.12.cloned.1.call-update) | async-done | bytes 1048592 | tf_op jit(solution)/shard_map/all_gather | solution.py:183
  174.3 1.5 copy.58
  175.8 82.8 %all-gather.8.cloned.1.call-done = bf16[4,2048,512]{2,1,0:T(8,128)(2,1)} async-done(((bf16[4,256,512]{2,1,0:T(8,128)(2,1)}), bf16[4,2048,512]{2,1,0:T(8,128)(2,1)}) %all-gather.8.cloned.1.call-update) | async-done | bytes 8388624 | tf_op jit(solution)/shard_map/all_gather | solution.py:41
  258.6 6.7 %fusion.7 = bf16[256,2048]{1,0:T(8,128)(2,1)} fusion(bf16[4,256,512]{2,1,0:T(8,128)(2,1)S(1)} %bitcast.185, bf16[4,2048,512]{2,1,0:T(8,128)(2,1)} %all-gather.8.cloned.1.call-done), kind=kOutput, calls=%fused_computation.15 | convolution fusion | flops 2148007936 | bytes 10485760 | tf_op jit(solution)/shard_map/dot_general | solution.py:185
  265.3 4.6 %all-to-all-start.1 = ((bf16[4,64,2048]{2,1,0:T(8,128)(2,1)}), bf16[4,64,2048]{2,1,0:T(8,128)(2,1)S(1)}, u32[]{:S(2)}, u32[]{:S(2)}) async-start(bf16[4,64,2048]{2,1,0:T(8,128)(2,1)} %bitcast.37), calls=%async_computation.2 | async-start | bytes 2097152 | tf_op jit(solution)/shard_map/all_to_all | solution.py:188
  269.9 2.9 multiply_convert_fusion
  272.8 1.4 copy.62
  274.2 15.0 %all-gather.10.cloned.1.call-done = bf16[2048,512]{0,1:T(8,128)(2,1)} async-done(((bf16[256,512]{0,1:T(8,128)(2,1)}), bf16[2048,512]{0,1:T(8,128)(2,1)}) %all-gather.10.cloned.1.call-update) | async-done | bytes 2097168 | tf_op jit(solution)/shard_map/all_gather | solution.py:184
  289.3 5.3 %convolution_convert_fusion = bf16[1024,512]{1,0:T(8,128)(2,1)S(1)} fusion(bf16[2048,1024]{1,0:T(8,128)(2,1)} %bitcast.47, bf16[2048,512]{0,1:T(8,128)(2,1)} %all-gather.10.cloned.1.call-done), kind=kOutput, calls=%fused_computation.19 | convolution fusion | flops 2148007936 | bytes 7340032 | tf_op jit(solution)/shard_map/dot_general | solution.py:189
  296.9 1.6 broadcast_in_dim.114
  (72 shorter events, 22.5 us)
Async XLA Ops:
  7.2 6.7 %copy-start = (s32[1,512]{1,0:T(1,128)S(1)}, s32[1,512]{1,0:T(1,128)}, u32[]{:S(2)}) copy-start(s32[1,512]{1,0:T(1,128)} %param.19) | copy-start | bytes 6148
  7.2 13.0 %copy-start.8 = (bf16[1,256,2048]{2,1,0:T(8,128)(2,1)S(1)}, bf16[1,256,2048]{2,1,0:T(8,128)(2,1)}, u32[]{:S(2)}) copy-start(bf16[1,256,2048]{2,1,0:T(8,128)(2,1)} %param.14) | copy-start | bytes 3145732
  7.2 85.9 %all-gather.6.cloned.1.call-start = ((), (), s32[]{:S(2)}) async-start(), calls=%async_computation.4 | async-start | bytes 5242880 | tf_op jit(solution)/shard_map/all_gather | solution.py:28
  7.9 133.9 %reduce-scatter.2.cloned.1.call-start = ((), (), s32[]{:S(2)}) async-start(), calls=%async_computation.5 | async-start | bytes 1572864 | tf_op jit(solution)/shard_map/reduce_scatter | solution.py:177
  15.8 8.0 %copy-start.7 = (bf16[1,256,2048]{2,1,0:T(8,128)(2,1)S(1)}, bf16[1,256,2048]{2,1,0:T(8,128)(2,1)}, u32[]{:S(2)}) copy-start(bf16[1,256,2048]{2,1,0:T(8,128)(2,1)} %param.15) | copy-start | bytes 3145732
  93.1 5.3 %copy-start.2 = (bf16[1,256,8192]{2,1,0:T(8,128)(2,1)S(1)}, bf16[1,256,8192]{2,1,0:T(8,128)(2,1)}, u32[]{:S(2)}) copy-start(bf16[1,256,8192]{2,1,0:T(8,128)(2,1)} %all-gather.6.cloned.1.call-done) | copy-start | bytes 12582916
  93.1 5.9 %copy-start.5 = (bf16[8192,256]{1,0:T(8,128)(2,1)S(1)}, bf16[8192,256]{1,0:T(8,128)(2,1)}, u32[]{:S(2)}) copy-start(bf16[8192,256]{1,0:T(8,128)(2,1)} %param.17) | copy-start | bytes 12582916
  111.3 1.8 copy-start.9
  118.2 2.0 copy-start.4
  125.1 28.6 %all-to-all-start = ((bf16[4,256,512]{2,1,0:T(8,128)(2,1)}), bf16[4,256,512]{2,1,0:T(8,128)(2,1)S(1)}, u32[]{:S(2)}, u32[]{:S(2)}) async-start(bf16[4,256,512]{2,1,0:T(8,128)(2,1)} %pad_maximum_fusion.1), calls=%async_computation.1 | async-start | bytes 2097152 | tf_op jit(solution)/shard_map/all_to_all | solution.py:40
  128.7 45.6 %all-gather.12.cloned.1.call-start = ((), (), s32[]{:S(2)}) async-start(), calls=%async_computation.8 | async-start | bytes 1310720 | tf_op jit(solution)/shard_map/all_gather | solution.py:183
  143.6 115.0 %all-gather.8.cloned.1.call-start = ((), (), s32[]{:S(2)}) async-start(), calls=%async_computation.6 | async-start | bytes 9437184 | tf_op jit(solution)/shard_map/all_gather | solution.py:41
  153.7 1.0 copy-start.6
  154.7 7.7 %copy-start.3 = (bf16[1,256,8192]{2,1,0:T(8,128)(2,1)S(1)}, bf16[1,256,8192]{2,1,0:T(8,128)(2,1)}, u32[]{:S(2)}) copy-start(bf16[1,256,8192]{2,1,0:T(8,128)(2,1)} %all-gather.6.cloned.1.call-done) | copy-start | bytes 12582916
  165.8 99.5 %all-to-all-start.2 = ((bf16[8,256,1024]{2,1,0:T(8,128)(2,1)}), bf16[8,256,1024]{2,1,0:T(8,128)(2,1)}, u32[]{:S(2)}, u32[]{:S(2)}) async-start(bf16[8,256,1024]{2,1,0:T(8,128)(2,1)} %fusion.9), calls=%async_computation.3 | async-start | bytes 8388608 | tf_op jit(solution)/shard_map/all_to_all | solution.py:43
  170.4 118.9 %all-gather.10.cloned.1.call-start = ((), (), s32[]{:S(2)}) async-start(), calls=%async_computation.7 | async-start | bytes 2359296 | tf_op jit(solution)/shard_map/all_gather | solution.py:184
  265.3 30.8 %all-to-all-start.1 = ((bf16[4,64,2048]{2,1,0:T(8,128)(2,1)}), bf16[4,64,2048]{2,1,0:T(8,128)(2,1)S(1)}, u32[]{:S(2)}, u32[]{:S(2)}) async-start(bf16[4,64,2048]{2,1,0:T(8,128)(2,1)} %bitcast.37), calls=%async_computation.2 | async-start | bytes 2097152 | tf_op jit(solution)/shard_map/all_to_all | solution.py:188
  289.3 9.2 %copy-start.1 = (s32[1,512]{1,0:T(1,128)S(1)}, s32[1,512]{1,0:T(1,128)}, u32[]{:S(2)}) copy-start(s32[1,512]{1,0:T(1,128)} %param.19) | copy-start | bytes 6148
Sparse Core Ops, SparseCore 0:
  9.6 83.4 all-gather.5
  122.9 18.9 reduce-scatter.1
  144.0 30.1 all-gather.11
  176.8 81.7 all-gather.7
  261.0 28.1 all-gather.9
